TPU v7x, 32 devices: a whole 2x2x4 slice. The times are simulated.
32 devices in a mesh: groups: 2 (over y), pool: 4 (over z), sub: 2 (over x), chip: 2 (over core).
Axes of the slice: x: 2, y: 2, z: 4, core: 2. Of those that a mesh axis runs over, the one named last changes fastest.
Arguments:
- hidden: bfloat16 [1024, 4096], P(('groups', 'pool', 'sub', 'chip')), parts along dimension 0, may hold values from -6 to 6
- query_weight_matrix: bfloat16 [4096, 4096], P(None, 'pool'), may hold values from -0.09375 to 0.09375
- adapter_down_weight: bfloat16 [64, 64, 4096], P('pool', None, ('sub', 'chip')), may hold values from -0.09375 to 0.09375
- adapter_up_weight: bfloat16 [64, 64, 4096], P('pool', None, ('sub', 'chip')), may hold values from -0.75 to 0.75
- adapter_index_rows: int32 [1024], P(('groups', 'pool', 'sub', 'chip')), parts along dimension 0, may hold values from 0 to 63, as said below
Outputs:
- query: bfloat16 [1024, 4096], P(('groups', 'pool', 'sub', 'chip')), parts along dimension 0
There are 2 independent parts, one for each index of `groups`. A program takes and returns all parts, laid end to end along the dimension named above; an argument that names none is the same for every part. Nothing has to cross between parts.
Inputs may be any that keep to these rules, and one draw needn't show every extreme that they name: A row's owner is adapter_index_rows // 16. In each aligned block of 32 rows (the rows of one device) at most 12 rows have one owner, and in every block some owner has exactly 12 rows.
All inputs are finite; a program needn't handle non-finite values.
Results may differ from a plain program's by a relative error of at most 0.0052.
Values may be sent and summed in bfloat16 or wider, within the bound.
A program may use at most 64 MiB of HBM per device.

v0:
```python
import jax
import jax.numpy as jnp
from jax import lax
from jax.sharding import PartitionSpec as P

ADAPTER_SCALE = 0.5


def owner_rank(owner, count):
    table = (owner[:, None] == jnp.arange(count, dtype=jnp.int32)[None, :]).astype(jnp.int32)
    running = jnp.cumsum(table, axis=0) - table
    return jnp.sum(running * table, axis=1)


def reduced_rank_term(incoming_rows, nearby_adapters, adapter_down_weight, adapter_up_weight):
    adapter_stack, rank_extent, portion_width = adapter_down_weight.shape
    flattened_down = adapter_down_weight.reshape(adapter_stack * rank_extent, portion_width)
    project = lax.dot_general(
        incoming_rows, flattened_down, (((1,), (1,)), ((), ())), preferred_element_type=jnp.float32
    )
    select = nearby_adapters[:, None] == jnp.arange(adapter_stack, dtype=jnp.int32)[None, :]
    partial_low = jnp.sum(
        project.reshape(-1, adapter_stack, rank_extent) * select[:, :, None].astype(jnp.float32),
        axis=1,
    )
    projected_down = lax.psum(partial_low, ("sub", "chip")).astype(jnp.bfloat16)
    spread = (select[:, :, None].astype(jnp.bfloat16) * projected_down[:, None, :]).reshape(
        -1, adapter_stack * rank_extent
    )
    flattened_up = adapter_up_weight.reshape(adapter_stack * rank_extent, portion_width)
    update_term = jnp.dot(spread, flattened_up, preferred_element_type=jnp.float32)
    return (ADAPTER_SCALE * update_term).astype(jnp.bfloat16)


def local(hidden, query_weight_matrix, adapter_down_weight, adapter_up_weight, adapter_index_rows):
    pools = lax.axis_size("pool")
    shards = lax.axis_size(("sub", "chip"))
    shard_index = lax.axis_index(("sub", "chip"))
    row_count, width = hidden.shape
    adapter_stack = adapter_down_weight.shape[0]
    portion_width = adapter_down_weight.shape[2]
    capacity = 2 + row_count // (pools - 1)
    nothing = jnp.zeros((), jnp.bfloat16)
    query_cols = jnp.dot(
        lax.all_gather(hidden, "pool", axis=0, tiled=True),
        query_weight_matrix,
        preferred_element_type=jnp.float32,
    ).astype(jnp.bfloat16)
    block_rows, block_adapters = (
        lax.all_gather(hidden, ("sub", "chip"), axis=0, tiled=True),
        lax.all_gather(adapter_index_rows, ("sub", "chip"), axis=0, tiled=True),
    )
    block_size = shards * row_count
    per_owner = shards * capacity
    combined_output = pools * per_owner
    owner = block_adapters // adapter_stack
    slot = owner * per_owner + owner_rank(owner, pools)
    slot_row = (
        jnp.full((combined_output,), -1, jnp.int32)
        .at[slot]
        .set(jnp.arange(block_size, dtype=jnp.int32))
    )
    filled = slot_row >= 0
    safe_row = jnp.maximum(slot_row, 0)
    my_slice = lax.dynamic_slice_in_dim(block_rows, shard_index * portion_width, portion_width, 1)
    send_rows = jnp.where(filled[:, None], jnp.take(my_slice, safe_row, axis=0), nothing)
    send_adapters = jnp.where(filled, jnp.take(block_adapters % adapter_stack, safe_row), 0)
    received_rows, received_adapters = (
        lax.all_to_all(
            send_rows.reshape(pools, per_owner, portion_width),
            "pool",
            split_axis=0,
            concat_axis=0,
            tiled=True,
        ),
        lax.all_to_all(
            send_adapters.reshape(pools, per_owner), "pool", split_axis=0, concat_axis=0, tiled=True
        ),
    )
    update_term = reduced_rank_term(
        received_rows.reshape(combined_output, portion_width),
        received_adapters.reshape(combined_output),
        adapter_down_weight,
        adapter_up_weight,
    )
    returned = lax.all_to_all(
        update_term.reshape(pools, per_owner, portion_width),
        "pool",
        split_axis=0,
        concat_axis=0,
        tiled=True,
    )
    delta_block = jnp.take(returned.reshape(combined_output, portion_width), slot, axis=0)
    delta_rows = lax.all_to_all(
        delta_block, ("sub", "chip"), split_axis=0, concat_axis=1, tiled=True
    )
    query = lax.all_to_all(query_cols, "pool", split_axis=0, concat_axis=1, tiled=True)
    return (query.astype(jnp.float32) + delta_rows.astype(jnp.float32)).astype(jnp.bfloat16)


def solution(mesh):
    in_specs = (
        P(("groups", "pool", "sub", "chip"), None),
        P(None, "pool"),
        P("pool", None, ("sub", "chip")),
        P("pool", None, ("sub", "chip")),
        P(("groups", "pool", "sub", "chip")),
    )
    out_specs = P(("groups", "pool", "sub", "chip"), None)
    return jax.shard_map(local, mesh=mesh, in_specs=in_specs, out_specs=out_specs, check_vma=False)
```

profile of v0, /device:TPU:0, one launch (start us, length us, event | category | flops | bytes accessed | tf_op | source)
XLA Modules:
  0.0 115.8 jit_solution(494919803565934389)
XLA Ops:
  6.5 0.7 all-gather.5.cloned.1.call-update
  7.3 1.2 %dynamic-slice = u32[1]{0:T(128)} dynamic-slice(u32[32]{0:T(128)} %constant.102, u32[]{:T(128)S(6)} %add.48), dynamic_slice_sizes={1} | dynamic-slice | bytes 12
  9.2 0.9 dynamic-update-slice
  10.0 6.3 %all-reduce = s32[128]{0:T(128)S(1)} all-reduce(s32[128]{0:T(128)S(1)} %dynamic-update-slice), channel_id=1, replica_groups=mesh['groups'=2,'pool'=4,'sub'=2,'chip'=2] {'sub','chip'}, use_global_device_ids=true, to_apply=%add | all-reduce | flops 128 | bytes 1024
  16.5 0.2 reduce_window_sum.11
  16.7 0.2 select_reduce_fusion
  16.9 1.0 scatter_custom_fusion
  17.9 1.6 %gather_fusion = s32[192]{0:T(256)S(1)} fusion(s32[128]{0:T(128)S(1)} %get-tuple-element.12, s32[1024]{0:T(1024)S(1)} %pad_clamp_fusion.1), kind=kCustom, calls=%fused_computation | custom fusion | bytes 2304 | tf_op jit(solution)/shard_map/jit(_take)/gather | solution.py:67
  19.4 0.7 all_to_all.32
  20.1 4.9 %all-to-all-start.1 = ((s32[4,1,48]{2,1,0:T(1,128)}), s32[4,1,48]{2,1,0:T(1,128)S(1)}, u32[]{:S(2)}, u32[]{:S(2)}) async-start(s32[4,1,48]{2,1,0:T(1,128)} %all_to_all.32), calls=%async_computation.1 | async-start | bytes 4096 | tf_op jit(solution)/shard_map/all_to_all | solution.py:76
  25.0 0.7 all-gather.3.cloned.1.call-update
  25.7 0.1 broadcast_in_dim.67
  25.9 2.5 %all-gather.5.cloned.1.call-done = bf16[128,4096]{1,0:T(8,128)(2,1)} async-done(((bf16[32,4096]{1,0:T(8,128)(2,1)}), bf16[128,4096]{1,0:T(8,128)(2,1)}) %all-gather.5.cloned.1.call-update) | async-done | bytes 1048592 | tf_op jit(solution)/shard_map/all_gather | solution.py:50
  28.4 1.0 constant_dynamic-slice_fusion
  29.3 1.0 gather_fusion.1
  30.4 0.9 select_select_fusion
  31.2 4.6 %all-to-all-start.2 = ((bf16[4,48,1024]{2,1,0:T(8,128)(2,1)}), bf16[4,48,1024]{2,1,0:T(8,128)(2,1)S(1)}, u32[]{:S(2)}, u32[]{:S(2)}) async-start(bf16[4,48,1024]{2,1,0:T(8,128)(2,1)} %select_select_fusion), calls=%async_computation.2 | async-start | bytes 786432 | tf_op jit(solution)/shard_map/all_to_all | solution.py:69
  35.8 0.5 broadcast.96
  36.3 0.7 reduce.3
  37.1 20.6 %all-to-all-done.2 = bf16[4,48,1024]{2,1,0:T(8,128)(2,1)S(1)} async-done(((bf16[4,48,1024]{2,1,0:T(8,128)(2,1)}), bf16[4,48,1024]{2,1,0:T(8,128)(2,1)S(1)}, u32[]{:S(2)}, u32[]{:S(2)}) %all-to-all-start.2) | async-done | bytes 393248 | tf_op jit(solution)/shard_map/all_to_all | solution.py:69
  57.7 2.3 %fusion.2 = f32[192,64]{0,1:T(8,128)S(1)} fusion(bf16[192,1024,1]{1,0,2:T(8,128)(2,1)S(1)} %bitcast.27, bf16[16,64,1024]{2,1,0:T(8,128)(2,1)} %param.7, f32[192,16]{0,1:T(8,128)S(1)} %get-tuple-element.11), kind=kOutput, calls=%fused_computation.8 | convolution fusion | flops 403034112 | bytes 2551808 | tf_op jit(solution)/shard_map/dot_general | solution.py:18
  60.1 11.1 %psum.7 = bf16[192,64]{0,1:T(8,128)(2,1)S(1)} all-reduce(f32[192,64]{0,1:T(8,128)S(1)} %fusion.2), channel_id=1, replica_groups=mesh['groups'=2,'pool'=4,'sub'=2,'chip'=2] {'sub','chip'}, use_global_device_ids=true, to_apply=%region_4.5 | all-reduce | flops 12288 | bytes 73728 | tf_op jit(solution)/shard_map/psum | solution.py:26
  71.2 1.4 %fusion.1 = bf16[192,1024]{1,0:T(8,128)(2,1)} fusion(bf16[16,64,1024]{2,1,0:T(8,128)(2,1)S(1)} %copy-done, bf16[192,64]{0,1:T(8,128)(2,1)S(1)} %psum.7, bf16[192,16]{0,1:T(8,128)(2,1)S(1)} %get-tuple-element.10), kind=kOutput, calls=%fused_computation.7 | convolution fusion | flops 403243008 | bytes 2521088 | tf_op jit(solution)/shard_map/dot_general | solution.py:31
  72.5 3.5 %all-to-all-start.3 = ((bf16[4,48,1024]{2,1,0:T(8,128)(2,1)}), bf16[4,48,1024]{2,1,0:T(8,128)(2,1)S(1)}, u32[]{:S(2)}, u32[]{:S(2)}) async-start(bf16[4,48,1024]{2,1,0:T(8,128)(2,1)} %bitcast.6), calls=%async_computation.3 | async-start | bytes 786432 | tf_op jit(solution)/shard_map/all_to_all | solution.py:86
  76.0 5.7 %convolution_convert_fusion = bf16[128,1024]{1,0:T(8,128)(2,1)} fusion(bf16[128,4096]{1,0:T(8,128)(2,1)} %all-gather.3.cloned.1.call-done, bf16[4096,1024]{1,0:T(8,128)(2,1)} %param.6), kind=kOutput, calls=%fused_computation.9 | convolution fusion | flops 1073872896 | bytes 9699328 | tf_op jit(solution)/shard_map/dot_general | solution.py:44
  81.7 5.7 %all-to-all-done.3 = bf16[4,48,1024]{2,1,0:T(8,128)(2,1)S(1)} async-done(((bf16[4,48,1024]{2,1,0:T(8,128)(2,1)}), bf16[4,48,1024]{2,1,0:T(8,128)(2,1)S(1)}, u32[]{:S(2)}, u32[]{:S(2)}) %all-to-all-start.3) | async-done | bytes 393248 | tf_op jit(solution)/shard_map/all_to_all | solution.py:86
  87.4 3.4 %all-to-all-start = ((bf16[4,32,1024]{2,1,0:T(8,128)(2,1)}), bf16[4,32,1024]{2,1,0:T(8,128)(2,1)S(1)}, u32[]{:S(2)}, u32[]{:S(2)}) async-start(bf16[4,32,1024]{2,1,0:T(8,128)(2,1)} %bitcast), calls=%async_computation | async-start | bytes 524288 | tf_op jit(solution)/shard_map/all_to_all | solution.py:97
  90.9 0.9 gather_fusion.2
  91.7 0.1 broadcast_select_fusion
  91.8 5.7 %all-to-all-done = bf16[4,32,1024]{2,1,0:T(8,128)(2,1)S(1)} async-done(((bf16[4,32,1024]{2,1,0:T(8,128)(2,1)}), bf16[4,32,1024]{2,1,0:T(8,128)(2,1)S(1)}, u32[]{:S(2)}, u32[]{:S(2)}) %all-to-all-start) | async-done | bytes 262176 | tf_op jit(solution)/shard_map/all_to_all | solution.py:97
  97.5 10.6 %all_to_all.42 = bf16[4,32,1024]{2,1,0:T(8,128)(2,1)S(1)} all-to-all(bf16[4,32,1024]{2,1,0:T(8,128)(2,1)S(1)} %broadcast_select_fusion), channel_id=1, replica_groups=mesh['groups'=2,'pool'=4,'sub'=2,'chip'=2] {'sub','chip'}, dimensions={0} | all-to-all | bytes 524288 | tf_op jit(solution)/shard_map/all_to_all | solution.py:94
  108.2 0.7 copy.11
  (20 shorter events, 0.5 us)
Async XLA Ops:
  6.5 64.6 %copy-start = (bf16[16,64,1024]{2,1,0:T(8,128)(2,1)S(1)}, bf16[16,64,1024]{2,1,0:T(8,128)(2,1)}, u32[]{:S(2)}) copy-start(bf16[16,64,1024]{2,1,0:T(8,128)(2,1)} %param.8) | copy-start | bytes 6291460
  6.5 21.8 %all-gather.5.cloned.1.call-start = ((), (), s32[]{:S(2)}) async-start(), calls=%async_computation.6 | async-start | bytes 1310720 | tf_op jit(solution)/shard_map/all_gather | solution.py:50
  20.1 11.1 %all-to-all-start.1 = ((s32[4,1,48]{2,1,0:T(1,128)}), s32[4,1,48]{2,1,0:T(1,128)S(1)}, u32[]{:S(2)}, u32[]{:S(2)}) async-start(s32[4,1,48]{2,1,0:T(1,128)} %all_to_all.32), calls=%async_computation.1 | async-start | bytes 4096 | tf_op jit(solution)/shard_map/all_to_all | solution.py:76
  25.0 51.0 %all-gather.3.cloned.1.call-start = ((), (), s32[]{:S(2)}) async-start(), calls=%async_computation.5 | async-start | bytes 1310720 | tf_op jit(solution)/shard_map/all_gather | solution.py:45
  31.2 26.5 %all-to-all-start.2 = ((bf16[4,48,1024]{2,1,0:T(8,128)(2,1)}), bf16[4,48,1024]{2,1,0:T(8,128)(2,1)S(1)}, u32[]{:S(2)}, u32[]{:S(2)}) async-start(bf16[4,48,1024]{2,1,0:T(8,128)(2,1)} %select_select_fusion), calls=%async_computation.2 | async-start | bytes 786432 | tf_op jit(solution)/shard_map/all_to_all | solution.py:69
  72.5 14.8 %all-to-all-start.3 = ((bf16[4,48,1024]{2,1,0:T(8,128)(2,1)}), bf16[4,48,1024]{2,1,0:T(8,128)(2,1)S(1)}, u32[]{:S(2)}, u32[]{:S(2)}) async-start(bf16[4,48,1024]{2,1,0:T(8,128)(2,1)} %bitcast.6), calls=%async_computation.3 | async-start | bytes 786432 | tf_op jit(solution)/shard_map/all_to_all | solution.py:86
  87.4 10.2 %all-to-all-start = ((bf16[4,32,1024]{2,1,0:T(8,128)(2,1)}), bf16[4,32,1024]{2,1,0:T(8,128)(2,1)S(1)}, u32[]{:S(2)}, u32[]{:S(2)}) async-start(bf16[4,32,1024]{2,1,0:T(8,128)(2,1)} %bitcast), calls=%async_computation | async-start | bytes 524288 | tf_op jit(solution)/shard_map/all_to_all | solution.py:97
Sparse Core Ops, SparseCore 0:
  8.9 19.4 all-gather.4
  29.9 35.1 all-gather.2
where the time goes:
time: 116 us
  waiting for transfers between devices  35.9 us (31%)
  blocking collectives  28.1 us (24%)
  starting transfers between devices  16.3 us (14%)
  between operations  14.2 us (12%)
  local copies, waits for them, and re-layouts  9.72 us (8%)
  matrix products  9.37 us (8%)
  other arithmetic  2.18 us (2%)
    all_to_all x1, waiting for transfers between devices, local(): lax.all_to_all(send_rows.reshape(pools, per_owner, portion_width), 'pool'...  20.6 us
    psum x1, blocking collectives, reduced_rank_term(): projected_down = lax.psum(partial_low, ('sub', 'chip')).astype(jnp.bfloat16)  11.1 us
    all_to_all x1, blocking collectives, local(): lax.all_to_all(delta_block, ('sub', 'chip'), split_axis=0, concat_axis=1,...  10.6 us
    unnamed x1, blocking collectives  6.35 us
    all_to_all x1, waiting for transfers between devices, local(): lax.all_to_all(query_cols, 'pool', split_axis=0, concat_axis=1, tiled=True)  5.69 us
    dot_general x1, matrix products, local(): jnp.dot(lax.all_gather(hidden, 'pool', axis=0, tiled=True), query_weight_...  5.68 us
    all_to_all x1, waiting for transfers between devices, local(): lax.all_to_all(update_term.reshape(pools, per_owner, portion_width), 'poo...  5.67 us
    all_to_all x1, starting transfers between devices, local(): lax.all_to_all(send_adapters.reshape(pools, per_owner), 'pool', split_axi...  4.87 us
  transfers between devices with their start and end apart: 6, of which 4 were waited for; matrix products, arithmetic and copies ran while one was open for 17% of the time, Pallas kernels for 0%

commit v1 on v0

--- a/solution.py
+++ b/solution.py
@@ -4,6 +4,17 @@
 from jax.sharding import PartitionSpec as P
 
 ADAPTER_SCALE = 0.5
+
+
+def in_blocks(x, dim, length):
+    before, after = (x.shape[:dim], x.shape[dim + 1 :])
+    return jnp.moveaxis(x.reshape(*before, length, -1, *after), dim, 0)
+
+
+def joined_along(parts, dim):
+    parts = jnp.moveaxis(parts, 0, dim)
+    shape = parts.shape
+    return parts.reshape(*shape[:dim], shape[dim] * shape[dim + 1], *shape[dim + 2 :])
 
 
 def owner_rank(owner, count):
@@ -94,7 +105,16 @@
     delta_rows = lax.all_to_all(
         delta_block, ("sub", "chip"), split_axis=0, concat_axis=1, tiled=True
     )
-    query = lax.all_to_all(query_cols, "pool", split_axis=0, concat_axis=1, tiled=True)
+    devices, here = (lax.axis_size("pool"), lax.axis_index("pool"))
+    blocks = in_blocks(query_cols, 0, devices)
+    gathered = [blocks[here]]
+    for step in range(1, devices):
+        sent = blocks[(here + step) % devices]
+        gathered.append(
+            lax.ppermute(sent, "pool", [(i, (i + step) % devices) for i in range(devices)])
+        )
+    blocks = jnp.stack(gathered)[(here - jnp.arange(devices)) % devices]
+    query = joined_along(blocks, 1)
     return (query.astype(jnp.float32) + delta_rows.astype(jnp.float32)).astype(jnp.bfloat16)
 
 

time: 116 us -> 110 us (0.948)
  blocking collectives: 28.1 us -> 17.4 us
  starting transfers between devices: 16.3 us -> 21.3 us
    all_to_all x1 -> x0, blocking collectives: 10.6 us -> none  [local(): lax.all_to_all(delta_block, ('sub', 'chip'), split_axis=0, concat_axis=1,...]
    ppermute x0 -> x3, starting transfers between devices: none -> 4.94 us  [local(): lax.ppermute(sent, 'pool', [(i, (i + step) % devices) for i in range(devi...]
  transfers between devices with their start and end apart: 6 -> 9, of which waited for: 4 -> 4; matrix products, arithmetic and copies ran while one was open for 17% -> 19% of each run, Pallas kernels for 0% -> 0%
where the time goes in v1:
time: 110 us
  waiting for transfers between devices  35.1 us (32%)
  starting transfers between devices  21.3 us (19%)
  blocking collectives  17.4 us (16%)
  between operations  14.3 us (13%)
  local copies, waits for them, and re-layouts  10.3 us (9%)
  matrix products  8.69 us (8%)
  other arithmetic  2.95 us (3%)
    all_to_all x1, waiting for transfers between devices, local(): lax.all_to_all(send_rows.reshape(pools, per_owner, portion_width), 'pool'...  20.5 us
    psum x1, blocking collectives, reduced_rank_term(): projected_down = lax.psum(partial_low, ('sub', 'chip')).astype(jnp.bfloat16)  11.1 us
    unnamed x1, blocking collectives  6.35 us
    all_to_all x1, waiting for transfers between devices, local(): lax.all_to_all(delta_block, ('sub', 'chip'), split_axis=0, concat_axis=1,...  5.34 us
    all_to_all x1, waiting for transfers between devices, local(): lax.all_to_all(update_term.reshape(pools, per_owner, portion_width), 'poo...  5.28 us
    dot_general x1, matrix products, local(): jnp.dot(lax.all_gather(hidden, 'pool', axis=0, tiled=True), query_weight_...  4.97 us
    ppermute x3, starting transfers between devices, local(): lax.ppermute(sent, 'pool', [(i, (i + step) % devices) for i in range(devi...  4.94 us
    all_to_all x1, starting transfers between devices, local(): lax.all_to_all(send_adapters.reshape(pools, per_owner), 'pool', split_axi...  4.87 us
  transfers between devices with their start and end apart: 9, of which 4 were waited for; matrix products, arithmetic and copies ran while one was open for 19% of the time, Pallas kernels for 0%

profile of v1, /device:TPU:0, one launch (start us, length us, event | category | flops | bytes accessed | tf_op | source)
XLA Modules:
  0.0 110.0 jit_solution(9752463077464793776)
XLA Ops:
  6.5 0.7 all-gather.5.cloned.1.call-update
  7.3 1.2 %dynamic-slice = u32[1]{0:T(128)} dynamic-slice(u32[32]{0:T(128)} %constant.138, u32[]{:T(128)S(6)} %add.114), dynamic_slice_sizes={1} | dynamic-slice | bytes 12
  9.2 0.9 dynamic-update-slice
  10.0 6.3 %all-reduce = s32[128]{0:T(128)S(1)} all-reduce(s32[128]{0:T(128)S(1)} %dynamic-update-slice), channel_id=1, replica_groups=mesh['groups'=2,'pool'=4,'sub'=2,'chip'=2] {'sub','chip'}, use_global_device_ids=true, to_apply=%add | all-reduce | flops 128 | bytes 1024
  16.5 0.2 reduce_window_sum.11
  16.9 1.0 scatter_custom_fusion
  17.9 1.6 %gather_fusion.1 = s32[192]{0:T(256)S(1)} fusion(s32[128]{0:T(128)S(1)} %get-tuple-element.16, s32[1024]{0:T(1024)S(1)} %pad_clamp_fusion.1), kind=kCustom, calls=%fused_computation.1 | custom fusion | bytes 2304 | tf_op jit(solution)/shard_map/jit(_take)/gather | solution.py:78
  19.4 0.7 all_to_all.20
  20.1 4.9 %all-to-all-start = ((s32[4,1,48]{2,1,0:T(1,128)}), s32[4,1,48]{2,1,0:T(1,128)S(1)}, u32[]{:S(2)}, u32[]{:S(2)}) async-start(s32[4,1,48]{2,1,0:T(1,128)} %all_to_all.20), calls=%async_computation | async-start | bytes 4096 | tf_op jit(solution)/shard_map/all_to_all | solution.py:87
  25.0 0.7 all-gather.3.cloned.1.call-update
  25.9 2.5 %all-gather.5.cloned.1.call-done = bf16[128,4096]{1,0:T(8,128)(2,1)} async-done(((bf16[32,4096]{1,0:T(8,128)(2,1)}), bf16[128,4096]{1,0:T(8,128)(2,1)}) %all-gather.5.cloned.1.call-update) | async-done | bytes 1048592 | tf_op jit(solution)/shard_map/all_gather | solution.py:61
  28.4 1.0 constant_dynamic-slice_fusion
  29.3 1.0 gather_fusion.2
  30.4 0.9 select_select_fusion
  31.2 4.6 %all-to-all-start.1 = ((bf16[4,48,1024]{2,1,0:T(8,128)(2,1)}), bf16[4,48,1024]{2,1,0:T(8,128)(2,1)S(1)}, u32[]{:S(2)}, u32[]{:S(2)}) async-start(bf16[4,48,1024]{2,1,0:T(8,128)(2,1)} %select_select_fusion), calls=%async_computation.1 | async-start | bytes 786432 | tf_op jit(solution)/shard_map/all_to_all | solution.py:80
  36.0 0.5 broadcast.172
  36.5 0.7 reduce.3
  37.2 20.5 %all-to-all-done.1 = bf16[4,48,1024]{2,1,0:T(8,128)(2,1)S(1)} async-done(((bf16[4,48,1024]{2,1,0:T(8,128)(2,1)}), bf16[4,48,1024]{2,1,0:T(8,128)(2,1)S(1)}, u32[]{:S(2)}, u32[]{:S(2)}) %all-to-all-start.1) | async-done | bytes 393248 | tf_op jit(solution)/shard_map/all_to_all | solution.py:80
  57.7 2.3 %fusion.2 = f32[192,64]{0,1:T(8,128)S(1)} fusion(bf16[192,1024,1]{1,0,2:T(8,128)(2,1)S(1)} %bitcast.39, bf16[16,64,1024]{2,1,0:T(8,128)(2,1)} %param.7, f32[192,16]{0,1:T(8,128)S(1)} %get-tuple-element.15), kind=kOutput, calls=%fused_computation.9 | convolution fusion | flops 403034112 | bytes 2551808 | tf_op jit(solution)/shard_map/dot_general | solution.py:29
  60.1 11.1 %psum.7 = bf16[192,64]{0,1:T(8,128)(2,1)S(1)} all-reduce(f32[192,64]{0,1:T(8,128)S(1)} %fusion.2), channel_id=1, replica_groups=mesh['groups'=2,'pool'=4,'sub'=2,'chip'=2] {'sub','chip'}, use_global_device_ids=true, to_apply=%region_4.5 | all-reduce | flops 12288 | bytes 73728 | tf_op jit(solution)/shard_map/psum | solution.py:37
  71.2 1.4 %fusion.1 = bf16[192,1024]{1,0:T(8,128)(2,1)} fusion(bf16[16,64,1024]{2,1,0:T(8,128)(2,1)S(1)} %copy-done, bf16[192,64]{0,1:T(8,128)(2,1)S(1)} %psum.7, bf16[192,16]{0,1:T(8,128)(2,1)S(1)} %get-tuple-element.14), kind=kOutput, calls=%fused_computation.8 | convolution fusion | flops 403243008 | bytes 2521088 | tf_op jit(solution)/shard_map/dot_general | solution.py:42
  72.5 3.5 %all-to-all-start.2 = ((bf16[4,48,1024]{2,1,0:T(8,128)(2,1)}), bf16[4,48,1024]{2,1,0:T(8,128)(2,1)S(1)}, u32[]{:S(2)}, u32[]{:S(2)}) async-start(bf16[4,48,1024]{2,1,0:T(8,128)(2,1)} %bitcast.13), calls=%async_computation.2 | async-start | bytes 786432 | tf_op jit(solution)/shard_map/all_to_all | solution.py:97
  76.0 5.0 %convolution_convert_fusion = bf16[128,1024]{1,0:T(8,128)(2,1)S(1)} fusion(bf16[128,4096]{1,0:T(8,128)(2,1)} %all-gather.3.cloned.1.call-done, bf16[4096,1024]{1,0:T(8,128)(2,1)} %param.6), kind=kOutput, calls=%fused_computation.10 | convolution fusion | flops 1073872896 | bytes 9699328 | tf_op jit(solution)/shard_map/dot_general | solution.py:55
  81.1 3.8 %collective-permute-start.2 = (bf16[32,1024]{1,0:T(8,128)(2,1)S(1)}, bf16[32,1024]{1,0:T(8,128)(2,1)S(1)}, u32[]{:S(2)}, u32[]{:S(2)}) collective-permute-start(bf16[32,1024]{1,0:T(8,128)(2,1)S(1)} %get-tuple-element.11), channel_id=1, source_target_pairs={{0,12},{4,0},{8,4},{12,8},{1,13},{5,1},{9,5},{13,9},{2,14},{6,2},{... | collective-permute-start | bytes 196616 | tf_op jit(solution)/shard_map/ppermute | solution.py:114
  84.9 1.1 %collective-permute-start = (bf16[32,1024]{1,0:T(8,128)(2,1)S(1)}, bf16[32,1024]{1,0:T(8,128)(2,1)S(1)}, u32[]{:S(2)}, u32[]{:S(2)}) collective-permute-start(bf16[32,1024]{1,0:T(8,128)(2,1)S(1)} %get-tuple-element.13), channel_id=1, source_target_pairs={{0,4},{4,8},{8,12},{12,0},{1,5},{5,9},{9,13},{13,1},{2,6},{6,10},{... | collective-permute-start | bytes 196616 | tf_op jit(solution)/shard_map/ppermute | solution.py:114
  86.0 5.3 %all-to-all-done.2 = bf16[4,48,1024]{2,1,0:T(8,128)(2,1)S(1)} async-done(((bf16[4,48,1024]{2,1,0:T(8,128)(2,1)}), bf16[4,48,1024]{2,1,0:T(8,128)(2,1)S(1)}, u32[]{:S(2)}, u32[]{:S(2)}) %all-to-all-start.2) | async-done | bytes 393248 | tf_op jit(solution)/shard_map/all_to_all | solution.py:97
  91.3 0.9 gather_fusion.3
  92.1 0.8 broadcast_select_fusion
  92.9 3.4 %all-to-all-start.3 = ((bf16[4,32,1024]{2,1,0:T(8,128)(2,1)}), bf16[4,32,1024]{2,1,0:T(8,128)(2,1)S(1)}, u32[]{:S(2)}, u32[]{:S(2)}) async-start(bf16[4,32,1024]{2,1,0:T(8,128)(2,1)} %broadcast_select_fusion), calls=%async_computation.3 | async-start | bytes 524288 | tf_op jit(solution)/shard_map/all_to_all | solution.py:105
  96.4 0.6 gather_fusion
  97.0 5.3 %all-to-all-done.3 = bf16[4,32,1024]{2,1,0:T(8,128)(2,1)S(1)} async-done(((bf16[4,32,1024]{2,1,0:T(8,128)(2,1)}), bf16[4,32,1024]{2,1,0:T(8,128)(2,1)S(1)}, u32[]{:S(2)}, u32[]{:S(2)}) %all-to-all-start.3) | async-done | bytes 262176 | tf_op jit(solution)/shard_map/all_to_all | solution.py:105
  102.4 0.7 copy.11
  (30 shorter events, 0.8 us)
Async XLA Ops:
  6.5 64.6 %copy-start = (bf16[16,64,1024]{2,1,0:T(8,128)(2,1)S(1)}, bf16[16,64,1024]{2,1,0:T(8,128)(2,1)}, u32[]{:S(2)}) copy-start(bf16[16,64,1024]{2,1,0:T(8,128)(2,1)} %param.8) | copy-start | bytes 6291460
  6.5 21.8 %all-gather.5.cloned.1.call-start = ((), (), s32[]{:S(2)}) async-start(), calls=%async_computation.5 | async-start | bytes 1310720 | tf_op jit(solution)/shard_map/all_gather | solution.py:61
  20.1 11.1 %all-to-all-start = ((s32[4,1,48]{2,1,0:T(1,128)}), s32[4,1,48]{2,1,0:T(1,128)S(1)}, u32[]{:S(2)}, u32[]{:S(2)}) async-start(s32[4,1,48]{2,1,0:T(1,128)} %all_to_all.20), calls=%async_computation | async-start | bytes 4096 | tf_op jit(solution)/shard_map/all_to_all | solution.py:87
  25.0 51.1 %all-gather.3.cloned.1.call-start = ((), (), s32[]{:S(2)}) async-start(), calls=%async_computation.4 | async-start | bytes 1310720 | tf_op jit(solution)/shard_map/all_gather | solution.py:56
  31.2 26.5 %all-to-all-start.1 = ((bf16[4,48,1024]{2,1,0:T(8,128)(2,1)}), bf16[4,48,1024]{2,1,0:T(8,128)(2,1)S(1)}, u32[]{:S(2)}, u32[]{:S(2)}) async-start(bf16[4,48,1024]{2,1,0:T(8,128)(2,1)} %select_select_fusion), calls=%async_computation.1 | async-start | bytes 786432 | tf_op jit(solution)/shard_map/all_to_all | solution.py:80
  72.5 18.7 %all-to-all-start.2 = ((bf16[4,48,1024]{2,1,0:T(8,128)(2,1)}), bf16[4,48,1024]{2,1,0:T(8,128)(2,1)S(1)}, u32[]{:S(2)}, u32[]{:S(2)}) async-start(bf16[4,48,1024]{2,1,0:T(8,128)(2,1)} %bitcast.13), calls=%async_computation.2 | async-start | bytes 786432 | tf_op jit(solution)/shard_map/all_to_all | solution.py:97
  81.1 15.3 %collective-permute-start.2 = (bf16[32,1024]{1,0:T(8,128)(2,1)S(1)}, bf16[32,1024]{1,0:T(8,128)(2,1)S(1)}, u32[]{:S(2)}, u32[]{:S(2)}) collective-permute-start(bf16[32,1024]{1,0:T(8,128)(2,1)S(1)} %get-tuple-element.11), channel_id=1, source_target_pairs={{0,12},{4,0},{8,4},{12,8},{1,13},{5,1},{9,5},{13,9},{2,14},{6,2},{... | collective-permute-start | bytes 196616 | tf_op jit(solution)/shard_map/ppermute | solution.py:114
  84.9 11.5 %collective-permute-start.1 = (bf16[32,1024]{1,0:T(8,128)(2,1)S(1)}, bf16[32,1024]{1,0:T(8,128)(2,1)S(1)}, u32[]{:S(2)}, u32[]{:S(2)}) collective-permute-start(bf16[32,1024]{1,0:T(8,128)(2,1)S(1)} %get-tuple-element.12), channel_id=1, source_target_pairs={{0,8},{4,12},{8,0},{12,4},{1,9},{5,13},{9,1},{13,5},{2,10},{6,14},... | collective-permute-start | bytes 196616 | tf_op jit(solution)/shard_map/ppermute | solution.py:114
  84.9 11.5 %collective-permute-start = (bf16[32,1024]{1,0:T(8,128)(2,1)S(1)}, bf16[32,1024]{1,0:T(8,128)(2,1)S(1)}, u32[]{:S(2)}, u32[]{:S(2)}) collective-permute-start(bf16[32,1024]{1,0:T(8,128)(2,1)S(1)} %get-tuple-element.13), channel_id=1, source_target_pairs={{0,4},{4,8},{8,12},{12,0},{1,5},{5,9},{9,13},{13,1},{2,6},{6,10},{... | collective-permute-start | bytes 196616 | tf_op jit(solution)/shard_map/ppermute | solution.py:114
  92.9 9.4 %all-to-all-start.3 = ((bf16[4,32,1024]{2,1,0:T(8,128)(2,1)}), bf16[4,32,1024]{2,1,0:T(8,128)(2,1)S(1)}, u32[]{:S(2)}, u32[]{:S(2)}) async-start(bf16[4,32,1024]{2,1,0:T(8,128)(2,1)} %broadcast_select_fusion), calls=%async_computation.3 | async-start | bytes 524288 | tf_op jit(solution)/shard_map/all_to_all | solution.py:105
Sparse Core Ops, SparseCore 0:
  8.9 19.4 all-gather.4
  29.9 35.1 all-gather.2
